TPU v7x, 128 devices: a whole 4x4x4 slice. The times are simulated.
128 devices in a mesh: row: 8 (over z, x_hi), col: 16 (over x_lo, y, core).
Axes of the slice: x: 4 (x_hi: 2, x_lo: 2; x = x_hi * 2 + x_lo), y: 4, z: 4, core: 2. Of those that a mesh axis runs over, the one named last changes fastest.
Arguments:
- embeddings: bfloat16 [32768, 768], P(('row', 'col'))
- spread: bfloat16 [32768], P(('row', 'col')), may hold values from 1 to 16
- features: bfloat16 [32768, 256], P(('row', 'col')), may hold values from -160 to 160
- block_list: int32 [256], replicated, may hold values from 0 to 63
- list_pairs: int32 [64, 64], replicated, may hold values from 0 to 1, as said below
Outputs:
- smoothed: float32 [32768, 256], P(('row', 'col'))
Inputs may be any that keep to these rules, and one draw needn't show every extreme that they name: `list_pairs`: symmetric, with ones on the diagonal.
All inputs are finite; a program needn't handle non-finite values.
Results may differ from a plain program's by a relative error of at most 0.0029.
Values may be sent and summed in bfloat16 or wider, within the bound.
A program may use at most 64 MiB of HBM per device.

v0:
```python
import math
import jax
import jax.numpy as jnp
from jax import lax
from jax.sharding import PartitionSpec as P

BLK = 128
LISTS = 64


def active_table(block_list, list_pairs, row_blocks, col_blocks):
    count = block_list.shape[0]
    lists_onehot = (block_list[:, None] == jnp.arange(LISTS, dtype=jnp.int32)[None, :]).astype(
        jnp.float32
    )
    pair_table = list_pairs.astype(jnp.float32)
    row_select = (row_blocks[:, None] == jnp.arange(count, dtype=jnp.int32)[None, :]).astype(
        jnp.float32
    )
    col_select = (col_blocks[:, None] == jnp.arange(count, dtype=jnp.int32)[None, :]).astype(
        jnp.float32
    )
    row_onehot = jnp.dot(row_select, lists_onehot, precision=lax.Precision.HIGHEST)
    col_onehot = jnp.dot(col_select, lists_onehot, precision=lax.Precision.HIGHEST)
    joined = jnp.dot(row_onehot, pair_table, precision=lax.Precision.HIGHEST)
    return jnp.dot(joined, col_onehot.T, precision=lax.Precision.HIGHEST)


def shards(embeddings, spread, features, block_list, list_pairs):
    rows_x, rows_beta = (
        lax.all_gather(embeddings, "col", axis=0, tiled=True),
        lax.all_gather(spread, "col", axis=0, tiled=True),
    )
    cols_x, cols_beta, cols_feat = (
        lax.all_gather(embeddings, "row", axis=0, tiled=True),
        lax.all_gather(spread, "row", axis=0, tiled=True),
        lax.all_gather(features, "row", axis=0, tiled=True),
    )
    own_count = embeddings.shape[0]
    col_size = lax.axis_size("col")
    row_index = lax.axis_index("row")
    col_index = lax.axis_index("col")
    total_rows = rows_x.shape[0]
    total_cols = cols_x.shape[0]
    row_ids = row_index * total_rows + jnp.arange(total_rows, dtype=jnp.int32)
    local_index = jnp.arange(total_cols, dtype=jnp.int32)
    col_ids = (
        local_index // own_count * col_size + col_index
    ) * own_count + local_index % own_count
    active = active_table(block_list, list_pairs, row_ids[::BLK] // BLK, col_ids[::BLK] // BLK)
    col_blocks = active.shape[1]
    row_norm = jnp.sum(jnp.square(rows_x.astype(jnp.float32)), axis=1)
    col_norm = jnp.sum(jnp.square(cols_x.astype(jnp.float32)), axis=1)
    row_bw = rows_beta.astype(jnp.float32)
    col_bw = cols_beta.astype(jnp.float32)

    def block_terms(start, size):
        row_emb = lax.dynamic_slice_in_dim(rows_x, start, size, 0)
        norm_part = lax.dynamic_slice_in_dim(row_norm, start, size, 0)
        beta_part = lax.dynamic_slice_in_dim(row_bw, start, size, 0)
        ids_part = lax.dynamic_slice_in_dim(row_ids, start, size, 0)
        inner = lax.dot_general(
            row_emb, cols_x, (((1,), (1,)), ((), ())), preferred_element_type=jnp.float32
        )
        dist = norm_part[:, None] + col_norm[None, :] - 2.0 * inner
        active_part = lax.dynamic_slice_in_dim(active, start // BLK, size // BLK, 0)
        expanded = jnp.broadcast_to(
            active_part[:, None, :, None], (size // BLK, BLK, col_blocks, BLK)
        )
        mask = expanded.reshape(size, total_cols) * (ids_part[:, None] != col_ids[None, :]).astype(
            jnp.float32
        )
        near = mask * jnp.exp(-beta_part[:, None] * dist)
        return (mask, dist, near)

    block_rows = math.gcd(total_rows, 512)
    starts = jnp.arange(total_rows // block_rows, dtype=jnp.int32) * block_rows
    row_partial = lax.map(
        lambda start: jnp.sum(block_terms(start, block_rows)[2], axis=1), starts
    ).reshape(total_rows)
    row_totals = lax.psum(row_partial, "col")
    own_totals = lax.dynamic_slice_in_dim(row_totals, col_index * own_count, own_count, 0)
    col_totals = lax.all_gather(own_totals, "row", axis=0, tiled=True)
    size = math.gcd(total_rows, 512)

    def one_block(begin):
        mask, dist, near = block_terms(begin, size)
        far = mask * jnp.exp(-col_bw[None, :] * dist)
        total_part = lax.dynamic_slice_in_dim(row_totals, begin, size, 0)
        weight = ((near / total_part[:, None] + far / col_totals[None, :]) * 0.5).astype(
            jnp.bfloat16
        )
        return jnp.dot(weight, cols_feat, preferred_element_type=jnp.float32)

    begins = 0 + jnp.arange(total_rows // size, dtype=jnp.int32) * size
    partial_out = lax.map(one_block, begins).reshape(total_rows, cols_feat.shape[1])
    summed = lax.psum(partial_out, "col")
    return lax.dynamic_slice_in_dim(summed, col_index * own_count, own_count, 0)


def solution(mesh):
    return jax.shard_map(
        shards,
        mesh=mesh,
        in_specs=(P(("row", "col"), None), P(("row", "col")), P(("row", "col"), None), P(), P()),
        out_specs=P(("row", "col"), None),
        check_vma=False,
    )
```

profile of v0, /device:TPU:1, one launch (start us, length us, event | category | flops | bytes accessed | tf_op | source)
XLA Modules:
  0.0 548.1 jit_solution(9659464464459559050)
XLA Ops:
  6.5 0.7 all-gather.9.cloned.1.call-update
  7.3 0.7 all-gather.7.cloned.1.call-update
  8.1 0.7 all-gather.11.cloned.1.call-update
  8.8 0.7 reshape.44
  9.5 21.2 %all-gather = bf16[16,1,256]{2,1,0:T(2,128)(2,1)S(1)} all-gather(bf16[1,1,256]{2,1,0:T(2,128)(2,1)S(1)} %reshape.44), channel_id=1, replica_groups=mesh['row'=8,'col'=16] {'col'}, dimensions={0}, use_global_device_ids=true | all-gather | bytes 8704 | tf_op jit(solution)/shard_map/all_gather | solution.py:32
  30.6 20.6 %all-gather.1 = bf16[8,1,256]{2,1,0:T(2,128)(2,1)S(1)} all-gather(bf16[1,1,256]{2,1,0:T(2,128)(2,1)S(1)} %reshape.44), channel_id=1, replica_groups=mesh['row'=8,'col'=16] {'row'}, dimensions={0}, use_global_device_ids=true | all-gather | bytes 4608 | tf_op jit(solution)/shard_map/all_gather | solution.py:36
  51.5 0.9 fusion.40
  52.4 0.9 fusion.41
  53.3 0.9 fusion.44
  54.4 21.0 %all-gather.9.cloned.1.call-done = bf16[2048,768]{1,0:T(8,128)(2,1)} async-done(((bf16[256,768]{1,0:T(8,128)(2,1)}), bf16[2048,768]{1,0:T(8,128)(2,1)}) %all-gather.9.cloned.1.call-update) | async-done | bytes 3145744 | tf_op jit(solution)/shard_map/all_gather | solution.py:35
  75.3 2.7 multiply_reduce_fusion.1
  78.1 39.8 %all-gather.7.cloned.1.call-done = bf16[4096,768]{1,0:T(8,128)(2,1)} async-done(((bf16[256,768]{1,0:T(8,128)(2,1)}), bf16[4096,768]{1,0:T(8,128)(2,1)}) %all-gather.7.cloned.1.call-update) | async-done | bytes 6291472 | tf_op jit(solution)/shard_map/all_gather | solution.py:31
  117.9 4.1 multiply_reduce_fusion
  122.0 102.0 %while.26 = (s32[]{:T(128)}, f32[8,512]{1,0:T(8,128)S(1)}, s32[8]{0:T(128)S(1)}, s32[4096]{0:T(1024)S(1)}, f32[32,16]{1,0:T(8,128)S(1)}, /*index=5*/f32[4096]{0:...) while((s32[]{:T(128)}, f32[8,512]{1,0:T(8,128)S(1)}, ...), condition=%wide.region_4.5_spmd.clone, body=%wide.region_2.4_spmd.clone.sunk | while | flops 1619034112 | bytes 12371102 | solution.py:78
  122.0 0.6 dynamic_slice.126
  125.1 2.4 broadcast_in_dim.65
  129.0 5.8 %fusion.78 = f32[512]{0:T(512)S(1)} fusion(f32[64,8,16,128]{3,2,1,0:T(8,128)} %bitcast.66, bf16[2048,768]{1,0:T(8,128)(2,1)S(1)} %get-tuple-element.698, f32[2048]{0:T(1024)S(1)} %get-tuple-element.696, f32[512]{0:T(512)S(1)} %dynamic_slice.127, f32[512]{0:T(512)S(1)} %dynamic-slice_negate_fusion.4, s32[2048]{0:T(1024)S(1)} %fusion.77, ...), kind=kOutput, calls=%fused_computation.4.clone.1 | convolution fusion | flops 1619000832 | bytes 8151044 | tf_op jit(solution)/shard_map/while/body/eval_jaxpr/dot_general | solution.py:62
  134.8 0.6 dynamic_slice.126
  137.9 2.4 broadcast_in_dim.65
  141.8 5.7 %fusion.78 = f32[512]{0:T(512)S(1)} fusion(f32[64,8,16,128]{3,2,1,0:T(8,128)} %bitcast.66, bf16[2048,768]{1,0:T(8,128)(2,1)S(1)} %get-tuple-element.698, f32[2048]{0:T(1024)S(1)} %get-tuple-element.696, f32[512]{0:T(512)S(1)} %dynamic_slice.127, f32[512]{0:T(512)S(1)} %dynamic-slice_negate_fusion.4, s32[2048]{0:T(1024)S(1)} %fusion.77, ...), kind=kOutput, calls=%fused_computation.4.clone.1 | convolution fusion | flops 1619000832 | bytes 8151044 | tf_op jit(solution)/shard_map/while/body/eval_jaxpr/dot_general | solution.py:62
  147.6 0.6 dynamic_slice.126
  150.7 2.4 broadcast_in_dim.65
  154.6 5.7 %fusion.78 = f32[512]{0:T(512)S(1)} fusion(f32[64,8,16,128]{3,2,1,0:T(8,128)} %bitcast.66, bf16[2048,768]{1,0:T(8,128)(2,1)S(1)} %get-tuple-element.698, f32[2048]{0:T(1024)S(1)} %get-tuple-element.696, f32[512]{0:T(512)S(1)} %dynamic_slice.127, f32[512]{0:T(512)S(1)} %dynamic-slice_negate_fusion.4, s32[2048]{0:T(1024)S(1)} %fusion.77, ...), kind=kOutput, calls=%fused_computation.4.clone.1 | convolution fusion | flops 1619000832 | bytes 8151044 | tf_op jit(solution)/shard_map/while/body/eval_jaxpr/dot_general | solution.py:62
  160.3 0.6 dynamic_slice.126
  163.4 2.4 broadcast_in_dim.65
  167.3 5.7 %fusion.78 = f32[512]{0:T(512)S(1)} fusion(f32[64,8,16,128]{3,2,1,0:T(8,128)} %bitcast.66, bf16[2048,768]{1,0:T(8,128)(2,1)S(1)} %get-tuple-element.698, f32[2048]{0:T(1024)S(1)} %get-tuple-element.696, f32[512]{0:T(512)S(1)} %dynamic_slice.127, f32[512]{0:T(512)S(1)} %dynamic-slice_negate_fusion.4, s32[2048]{0:T(1024)S(1)} %fusion.77, ...), kind=kOutput, calls=%fused_computation.4.clone.1 | convolution fusion | flops 1619000832 | bytes 8151044 | tf_op jit(solution)/shard_map/while/body/eval_jaxpr/dot_general | solution.py:62
  173.1 0.6 dynamic_slice.126
  176.2 2.4 broadcast_in_dim.65
  180.1 5.7 %fusion.78 = f32[512]{0:T(512)S(1)} fusion(f32[64,8,16,128]{3,2,1,0:T(8,128)} %bitcast.66, bf16[2048,768]{1,0:T(8,128)(2,1)S(1)} %get-tuple-element.698, f32[2048]{0:T(1024)S(1)} %get-tuple-element.696, f32[512]{0:T(512)S(1)} %dynamic_slice.127, f32[512]{0:T(512)S(1)} %dynamic-slice_negate_fusion.4, s32[2048]{0:T(1024)S(1)} %fusion.77, ...), kind=kOutput, calls=%fused_computation.4.clone.1 | convolution fusion | flops 1619000832 | bytes 8151044 | tf_op jit(solution)/shard_map/while/body/eval_jaxpr/dot_general | solution.py:62
  185.8 0.6 dynamic_slice.126
  188.9 2.4 broadcast_in_dim.65
  192.8 5.7 %fusion.78 = f32[512]{0:T(512)S(1)} fusion(f32[64,8,16,128]{3,2,1,0:T(8,128)} %bitcast.66, bf16[2048,768]{1,0:T(8,128)(2,1)S(1)} %get-tuple-element.698, f32[2048]{0:T(1024)S(1)} %get-tuple-element.696, f32[512]{0:T(512)S(1)} %dynamic_slice.127, f32[512]{0:T(512)S(1)} %dynamic-slice_negate_fusion.4, s32[2048]{0:T(1024)S(1)} %fusion.77, ...), kind=kOutput, calls=%fused_computation.4.clone.1 | convolution fusion | flops 1619000832 | bytes 8151044 | tf_op jit(solution)/shard_map/while/body/eval_jaxpr/dot_general | solution.py:62
  198.5 0.6 dynamic_slice.126
  201.6 2.4 broadcast_in_dim.65
  205.5 5.7 %fusion.78 = f32[512]{0:T(512)S(1)} fusion(f32[64,8,16,128]{3,2,1,0:T(8,128)} %bitcast.66, bf16[2048,768]{1,0:T(8,128)(2,1)S(1)} %get-tuple-element.698, f32[2048]{0:T(1024)S(1)} %get-tuple-element.696, f32[512]{0:T(512)S(1)} %dynamic_slice.127, f32[512]{0:T(512)S(1)} %dynamic-slice_negate_fusion.4, s32[2048]{0:T(1024)S(1)} %fusion.77, ...), kind=kOutput, calls=%fused_computation.4.clone.1 | convolution fusion | flops 1619000832 | bytes 8151044 | tf_op jit(solution)/shard_map/while/body/eval_jaxpr/dot_general | solution.py:62
  211.3 0.6 dynamic_slice.126
  214.4 2.4 broadcast_in_dim.65
  218.3 5.7 %fusion.78 = f32[512]{0:T(512)S(1)} fusion(f32[64,8,16,128]{3,2,1,0:T(8,128)} %bitcast.66, bf16[2048,768]{1,0:T(8,128)(2,1)S(1)} %get-tuple-element.698, f32[2048]{0:T(1024)S(1)} %get-tuple-element.696, f32[512]{0:T(512)S(1)} %dynamic_slice.127, f32[512]{0:T(512)S(1)} %dynamic-slice_negate_fusion.4, s32[2048]{0:T(1024)S(1)} %fusion.77, ...), kind=kOutput, calls=%fused_computation.4.clone.1 | convolution fusion | flops 1619000832 | bytes 8151044 | tf_op jit(solution)/shard_map/while/body/eval_jaxpr/dot_general | solution.py:62
  224.0 51.3 %psum.14 = f32[4096]{0:T(1024)S(1)} all-reduce(f32[4096]{0:T(1024)S(1)} %bitcast.69), channel_id=1, replica_groups=mesh['row'=8,'col'=16] {'col'}, use_global_device_ids=true, to_apply=%region_5.6 | all-reduce | flops 4096 | bytes 32768 | tf_op jit(solution)/shard_map/psum | solution.py:81
  275.4 19.4 %all-gather.2 = f32[8,1,256]{2,1,0:T(1,128)S(1)} all-gather(f32[1,1,256]{2,1,0:T(1,128)S(1)} %bitcast.75), channel_id=1, replica_groups=mesh['row'=8,'col'=16] {'row'}, dimensions={0}, use_global_device_ids=true | all-gather | bytes 9216 | tf_op jit(solution)/shard_map/all_gather | solution.py:83
  294.8 114.9 %while.27 = (s32[]{:T(128)}, f32[8,512,256]{2,1,0:T(8,128)}, s32[8]{0:T(128)S(1)}, s32[4096]{0:T(1024)S(1)}, f32[32,16]{1,0:T(8,128)S(1)}, /*index=5*/f32[4096]{...) while((s32[]{:T(128)}, f32[8,512,256]{2,1,0:T(8,128)}, ...), condition=%wide.region_7.8_spmd.clone, body=%wide.region_6.7_spmd.clone.sunk | while | flops 2162196992 | bytes 13960894 | solution.py:96
  294.8 0.6 dynamic_slice.132
  297.7 2.4 broadcast_in_dim.66
  301.6 7.6 %fusion.83 = f32[8,512,256]{2,1,0:T(8,128)} fusion(f32[8,512,256]{2,1,0:T(8,128)} %get-tuple-element.730, s32[]{:T(128)} %get-tuple-element.729, bf16[2048,256]{1,0:T(8,128)(2,1)} %get-tuple-element.764, f32[64,8,16,128]{3,2,1,0:T(8,128)} %bitcast.65, bf16[2048,768]{1,0:T(8,128)(2,1)S(1)} %get-tuple-element.760, f32[2048]{0:T(1024)S(1)} %get-tuple-element.763, ...), kind=kOutput, calls=%fused_computation.28.clone.1 | convolution fusion | flops 2162163712 | bytes 9740804 | tf_op jit(solution)/shard_map/while/body/eval_jaxpr/dot_general | solution.py:93
  309.2 0.6 dynamic_slice.132
  312.0 2.4 broadcast_in_dim.66
  315.9 7.6 %fusion.83 = f32[8,512,256]{2,1,0:T(8,128)} fusion(f32[8,512,256]{2,1,0:T(8,128)} %get-tuple-element.730, s32[]{:T(128)} %get-tuple-element.729, bf16[2048,256]{1,0:T(8,128)(2,1)} %get-tuple-element.764, f32[64,8,16,128]{3,2,1,0:T(8,128)} %bitcast.65, bf16[2048,768]{1,0:T(8,128)(2,1)S(1)} %get-tuple-element.760, f32[2048]{0:T(1024)S(1)} %get-tuple-element.763, ...), kind=kOutput, calls=%fused_computation.28.clone.1 | convolution fusion | flops 2162163712 | bytes 9740804 | tf_op jit(solution)/shard_map/while/body/eval_jaxpr/dot_general | solution.py:93
  323.5 0.6 dynamic_slice.132
  326.4 2.4 broadcast_in_dim.66
  330.3 7.6 %fusion.83 = f32[8,512,256]{2,1,0:T(8,128)} fusion(f32[8,512,256]{2,1,0:T(8,128)} %get-tuple-element.730, s32[]{:T(128)} %get-tuple-element.729, bf16[2048,256]{1,0:T(8,128)(2,1)} %get-tuple-element.764, f32[64,8,16,128]{3,2,1,0:T(8,128)} %bitcast.65, bf16[2048,768]{1,0:T(8,128)(2,1)S(1)} %get-tuple-element.760, f32[2048]{0:T(1024)S(1)} %get-tuple-element.763, ...), kind=kOutput, calls=%fused_computation.28.clone.1 | convolution fusion | flops 2162163712 | bytes 9740804 | tf_op jit(solution)/shard_map/while/body/eval_jaxpr/dot_general | solution.py:93
  337.9 0.6 dynamic_slice.132
  340.7 2.4 broadcast_in_dim.66
  344.6 7.6 %fusion.83 = f32[8,512,256]{2,1,0:T(8,128)} fusion(f32[8,512,256]{2,1,0:T(8,128)} %get-tuple-element.730, s32[]{:T(128)} %get-tuple-element.729, bf16[2048,256]{1,0:T(8,128)(2,1)} %get-tuple-element.764, f32[64,8,16,128]{3,2,1,0:T(8,128)} %bitcast.65, bf16[2048,768]{1,0:T(8,128)(2,1)S(1)} %get-tuple-element.760, f32[2048]{0:T(1024)S(1)} %get-tuple-element.763, ...), kind=kOutput, calls=%fused_computation.28.clone.1 | convolution fusion | flops 2162163712 | bytes 9740804 | tf_op jit(solution)/shard_map/while/body/eval_jaxpr/dot_general | solution.py:93
  352.2 0.6 dynamic_slice.132
  355.1 2.4 broadcast_in_dim.66
  359.0 7.6 %fusion.83 = f32[8,512,256]{2,1,0:T(8,128)} fusion(f32[8,512,256]{2,1,0:T(8,128)} %get-tuple-element.730, s32[]{:T(128)} %get-tuple-element.729, bf16[2048,256]{1,0:T(8,128)(2,1)} %get-tuple-element.764, f32[64,8,16,128]{3,2,1,0:T(8,128)} %bitcast.65, bf16[2048,768]{1,0:T(8,128)(2,1)S(1)} %get-tuple-element.760, f32[2048]{0:T(1024)S(1)} %get-tuple-element.763, ...), kind=kOutput, calls=%fused_computation.28.clone.1 | convolution fusion | flops 2162163712 | bytes 9740804 | tf_op jit(solution)/shard_map/while/body/eval_jaxpr/dot_general | solution.py:93
  369.5 2.4 broadcast_in_dim.66
  373.4 7.7 %fusion.83 = f32[8,512,256]{2,1,0:T(8,128)} fusion(f32[8,512,256]{2,1,0:T(8,128)} %get-tuple-element.730, s32[]{:T(128)} %get-tuple-element.729, bf16[2048,256]{1,0:T(8,128)(2,1)} %get-tuple-element.764, f32[64,8,16,128]{3,2,1,0:T(8,128)} %bitcast.65, bf16[2048,768]{1,0:T(8,128)(2,1)S(1)} %get-tuple-element.760, f32[2048]{0:T(1024)S(1)} %get-tuple-element.763, ...), kind=kOutput, calls=%fused_computation.28.clone.1 | convolution fusion | flops 2162163712 | bytes 9740804 | tf_op jit(solution)/shard_map/while/body/eval_jaxpr/dot_general | solution.py:93
  383.9 2.4 broadcast_in_dim.66
  387.8 7.6 %fusion.83 = f32[8,512,256]{2,1,0:T(8,128)} fusion(f32[8,512,256]{2,1,0:T(8,128)} %get-tuple-element.730, s32[]{:T(128)} %get-tuple-element.729, bf16[2048,256]{1,0:T(8,128)(2,1)} %get-tuple-element.764, f32[64,8,16,128]{3,2,1,0:T(8,128)} %bitcast.65, bf16[2048,768]{1,0:T(8,128)(2,1)S(1)} %get-tuple-element.760, f32[2048]{0:T(1024)S(1)} %get-tuple-element.763, ...), kind=kOutput, calls=%fused_computation.28.clone.1 | convolution fusion | flops 2162163712 | bytes 9740804 | tf_op jit(solution)/shard_map/while/body/eval_jaxpr/dot_general | solution.py:93
  398.2 2.4 broadcast_in_dim.66
  402.1 7.6 %fusion.83 = f32[8,512,256]{2,1,0:T(8,128)} fusion(f32[8,512,256]{2,1,0:T(8,128)} %get-tuple-element.730, s32[]{:T(128)} %get-tuple-element.729, bf16[2048,256]{1,0:T(8,128)(2,1)} %get-tuple-element.764, f32[64,8,16,128]{3,2,1,0:T(8,128)} %bitcast.65, bf16[2048,768]{1,0:T(8,128)(2,1)S(1)} %get-tuple-element.760, f32[2048]{0:T(1024)S(1)} %get-tuple-element.763, ...), kind=kOutput, calls=%fused_computation.28.clone.1 | convolution fusion | flops 2162163712 | bytes 9740804 | tf_op jit(solution)/shard_map/while/body/eval_jaxpr/dot_general | solution.py:93
  409.7 130.2 %all-reduce.2.cloned.1.call-done = f32[4096,256]{1,0:T(8,128)} async-done(((f32[4096,256]{1,0:T(8,128)}), f32[4096,256]{1,0:T(8,128)}) %all-reduce.2.cloned.1.call-update) | async-done | bytes 4194320 | tf_op jit(solution)/shard_map/psum | solution.py:97
  539.9 1.7 constant_dynamic-slice_fusion.2
  (121 shorter events, 7.4 us)
Async XLA Ops:
  6.5 68.8 %all-gather.9.cloned.1.call-start = ((), (), s32[]{:S(2)}) async-start(), calls=%async_computation.1 | async-start | bytes 3538944 | tf_op jit(solution)/shard_map/all_gather | solution.py:35
  7.3 110.6 %all-gather.7.cloned.1.call-start = ((), (), s32[]{:S(2)}) async-start(), calls=%async_computation | async-start | bytes 6684672 | tf_op jit(solution)/shard_map/all_gather | solution.py:31
  8.0 286.8 %all-gather.11.cloned.1.call-start = ((), (), s32[]{:S(2)}) async-start(), calls=%async_computation.2 | async-start | bytes 1179648 | tf_op jit(solution)/shard_map/all_gather | solution.py:37
  8.7 531.2 %all-reduce.2.cloned.1.call-start = ((), (), s32[]{:S(2)}) async-start(), calls=%async_computation.3 | async-start | bytes 8388608 | tf_op jit(solution)/shard_map/psum | solution.py:97
  75.3 46.6 %copy-start = (bf16[2048,768]{1,0:T(8,128)(2,1)S(1)}, bf16[2048,768]{1,0:T(8,128)(2,1)}, u32[]{:S(2)}) copy-start(bf16[2048,768]{1,0:T(8,128)(2,1)} %all-gather.9.cloned.1.call-done) | copy-start | bytes 9437188
Sparse Core Ops, SparseCore 0:
  9.7 65.6 all-gather.8
  77.0 40.7 all-gather.6
  120.2 45.7 all-gather.10
  409.9 130.0 all-reduce.1
where the time goes:
time: 549 us; the launch traced here: 548 us
  waiting for transfers between devices  193 us (35%)
  blocking collectives  112 us (20%)
  matrix products  109 us (20%)
  loops' own time  57.7 us (11%)
  local copies, waits for them, and re-layouts  54 us (10%)
  between operations  13.2 us (2%)
  other arithmetic  8.3 us (2%)
    psum x1, waiting for transfers between devices, shards(): summed = lax.psum(partial_out, 'col')  130 us
    dot_general x8, matrix products, one_block(): return jnp.dot(weight, cols_feat, preferred_element_type=jnp.float32)  61 us
    psum x1, blocking collectives, shards(): row_totals = lax.psum(row_partial, 'col')  51.3 us
    dot_general x8, matrix products, block_terms(): lax.dot_general(row_emb, cols_x, (((1,), (1,)), ((), ())), preferred_elem...  45.4 us
    all_gather x1, waiting for transfers between devices, shards(): lax.all_gather(embeddings, 'col', axis=0, tiled=True)  39.8 us
    broadcast_in_dim x16, local copies, waits for them, and re-layouts, block_terms(): jnp.broadcast_to(active_part[:, None, :, None], (size // BLK, BLK, col_bl...  38.6 us
    another operation x1, loops' own time, shards(): lax.map(lambda start: jnp.sum(block_terms(start, block_rows)[2], axis=1),...  30.1 us
    another operation x1, loops' own time, shards(): lax.map(one_block, begins).reshape(total_rows, cols_feat.shape[1])  27.6 us
  transfers between devices with their start and end apart: 4, of which 3 were waited for; matrix products, arithmetic and copies ran while one was open for 15% of the time, Pallas kernels for 0%

commit v1 on v0

--- a/solution.py
+++ b/solution.py
@@ -27,8 +27,14 @@
 
 
 def shards(embeddings, spread, features, block_list, list_pairs):
+
+    def state_types_on(my_tile, which_dim):
+        step_out = jnp.stack(lax.axis_size("col") * [my_tile])
+        carry_out = lax.all_to_all(step_out, "col", 0, 0)
+        return jnp.concatenate(carry_out, axis=which_dim)
+
     rows_x, rows_beta = (
-        lax.all_gather(embeddings, "col", axis=0, tiled=True),
+        state_types_on(embeddings, which_dim=0),
         lax.all_gather(spread, "col", axis=0, tiled=True),
     )
     cols_x, cols_beta, cols_feat = (

time: 549 us -> 592 us (1.078)
  blocking collectives: 112 us -> 204 us
  waiting for transfers between devices: 193 us -> 134 us
  starting transfers between devices: 0.12 us -> 7.12 us
    all_gather x1, blocking collectives: 21.2 us -> 115 us  [shards(): lax.all_gather(spread, 'col', axis=0, tiled=True)]
    all_gather x1 -> x0, waiting for transfers between devices: 39.8 us -> none  [shards(): lax.all_gather(embeddings, 'col', axis=0, tiled=True)]
    all_gather x1, waiting for transfers between devices: 21 us -> 0.02 us  [shards(): lax.all_gather(embeddings, 'row', axis=0, tiled=True)]
    all_to_all x0 -> x1, starting transfers between devices: none -> 7.05 us  [state_types_on(): carry_out = lax.all_to_all(step_out, 'col', 0, 0)]
  transfers between devices with their start and end apart: 4 -> 4, of which waited for: 3 -> 1; matrix products, arithmetic and copies ran while one was open for 15% -> 14% of each run, Pallas kernels for 0% -> 0%
where the time goes in v1:
time: 592 us; the launch traced here: 590 us
  blocking collectives  204 us (34%)
  waiting for transfers between devices  134 us (23%)
  matrix products  107 us (18%)
  loops' own time  59.3 us (10%)
  local copies, waits for them, and re-layouts  57.5 us (10%)
  between operations  13.3 us (2%)
  other arithmetic  8.29 us (1%)
  starting transfers between devices  7.12 us (1%)
    psum x1, waiting for transfers between devices, shards(): summed = lax.psum(partial_out, 'col')  133 us
    all_gather x1, blocking collectives, shards(): lax.all_gather(spread, 'col', axis=0, tiled=True)  115 us
    dot_general x8, matrix products, one_block(): return jnp.dot(weight, cols_feat, preferred_element_type=jnp.float32)  60.9 us
    psum x1, blocking collectives, shards(): row_totals = lax.psum(row_partial, 'col')  52.4 us
    dot_general x8, matrix products, block_terms(): lax.dot_general(row_emb, cols_x, (((1,), (1,)), ((), ())), preferred_elem...  45.2 us
    broadcast_in_dim x16, local copies, waits for them, and re-layouts, block_terms(): jnp.broadcast_to(active_part[:, None, :, None], (size // BLK, BLK, col_bl...  37.7 us
    another operation x1, loops' own time, shards(): lax.map(lambda start: jnp.sum(block_terms(start, block_rows)[2], axis=1),...  29.8 us
    another operation x1, loops' own time, shards(): lax.map(one_block, begins).reshape(total_rows, cols_feat.shape[1])  29.6 us
  transfers between devices with their start and end apart: 4, of which 1 were waited for; matrix products, arithmetic and copies ran while one was open for 14% of the time, Pallas kernels for 0%

profile of v1, /device:TPU:1, one launch (start us, length us, event | category | flops | bytes accessed | tf_op | source)
XLA Modules:
  0.0 590.4 jit_solution(5398249389695579258)
XLA Ops:
  6.5 0.7 all-gather.6.cloned.1.call-update
  7.3 4.3 stack.2
  11.5 7.0 %all-to-all-start = ((bf16[16,256,768]{2,1,0:T(8,128)(2,1)}), bf16[16,256,768]{2,1,0:T(8,128)(2,1)}, u32[]{:S(2)}, u32[]{:S(2)}) async-start(bf16[16,256,768]{2,1,0:T(8,128)(2,1)} %stack.2), calls=%async_computation | async-start | bytes 12582912 | tf_op jit(solution)/shard_map/all_to_all | solution.py:33
  18.6 0.7 all-gather.8.cloned.1.call-update
  19.7 115.4 %all-gather = bf16[16,1,256]{2,1,0:T(2,128)(2,1)S(1)} all-gather(bf16[1,1,256]{2,1,0:T(2,128)(2,1)S(1)} %reshape.51), channel_id=1, replica_groups=mesh['row'=8,'col'=16] {'col'}, dimensions={0}, use_global_device_ids=true | all-gather | bytes 8704 | tf_op jit(solution)/shard_map/all_gather | solution.py:38
  135.0 21.0 %all-gather.1 = bf16[8,1,256]{2,1,0:T(2,128)(2,1)S(1)} all-gather(bf16[1,1,256]{2,1,0:T(2,128)(2,1)S(1)} %reshape.51), channel_id=1, replica_groups=mesh['row'=8,'col'=16] {'row'}, dimensions={0}, use_global_device_ids=true | all-gather | bytes 4608 | tf_op jit(solution)/shard_map/all_gather | solution.py:42
  156.1 0.2 fusion.40
  156.3 0.2 fusion.41
  156.9 2.7 multiply_reduce_fusion.1
  159.6 4.1 multiply_reduce_fusion
  163.7 101.3 %while.26 = (s32[]{:T(128)}, f32[8,512]{1,0:T(8,128)S(1)}, s32[8]{0:T(128)S(1)}, s32[4096]{0:T(1024)S(1)}, f32[32,16]{1,0:T(8,128)S(1)}, /*index=5*/f32[4096]{0:...) while((s32[]{:T(128)}, f32[8,512]{1,0:T(8,128)S(1)}, ...), condition=%wide.region_4.5_spmd.clone, body=%wide.region_2.4_spmd.clone.sunk | while | flops 1619034112 | bytes 12371102 | solution.py:84
  163.8 0.6 dynamic_slice.126
  166.9 2.4 broadcast_in_dim.65
  170.7 5.7 fusion.78
  176.4 0.6 dynamic_slice.126
  179.5 2.4 broadcast_in_dim.65
  183.4 5.7 fusion.78
  189.1 0.6 dynamic_slice.126
  192.2 2.4 broadcast_in_dim.65
  196.0 5.6 fusion.78
  201.7 0.6 dynamic_slice.126
  204.8 2.4 broadcast_in_dim.65
  208.7 5.6 fusion.78
  214.4 0.6 dynamic_slice.126
  217.5 2.4 broadcast_in_dim.65
  221.3 5.6 fusion.78
  227.1 0.6 dynamic_slice.126
  230.2 2.4 broadcast_in_dim.65
  234.0 5.6 fusion.78
  239.7 0.6 dynamic_slice.126
  242.8 2.4 broadcast_in_dim.65
  246.6 5.6 fusion.78
  252.4 0.6 dynamic_slice.126
  255.5 2.4 broadcast_in_dim.65
  259.3 5.6 fusion.78
  265.0 52.4 %psum.14 = f32[4096]{0:T(1024)S(1)} all-reduce(f32[4096]{0:T(1024)S(1)} %bitcast.74), channel_id=1, replica_groups=mesh['row'=8,'col'=16] {'col'}, use_global_device_ids=true, to_apply=%region_5.6 | all-reduce | flops 4096 | bytes 32768 | tf_op jit(solution)/shard_map/psum | solution.py:87
  317.5 14.8 %all-gather.2 = f32[8,1,256]{2,1,0:T(1,128)S(1)} all-gather(f32[1,1,256]{2,1,0:T(1,128)S(1)} %bitcast.80), channel_id=1, replica_groups=mesh['row'=8,'col'=16] {'row'}, dimensions={0}, use_global_device_ids=true | all-gather | bytes 9216 | tf_op jit(solution)/shard_map/all_gather | solution.py:89
  332.3 116.9 %while.27 = (s32[]{:T(128)}, f32[8,512,256]{2,1,0:T(8,128)}, s32[8]{0:T(128)S(1)}, s32[4096]{0:T(1024)S(1)}, f32[32,16]{1,0:T(8,128)S(1)}, /*index=5*/f32[4096]{...) while((s32[]{:T(128)}, f32[8,512,256]{2,1,0:T(8,128)}, ...), condition=%wide.region_7.8_spmd.clone, body=%wide.region_6.7_spmd.clone.sunk | while | flops 2162196992 | bytes 13960894 | solution.py:102
  332.3 0.6 dynamic_slice.132
  335.4 2.4 broadcast_in_dim.66
  339.3 7.6 %fusion.83 = f32[8,512,256]{2,1,0:T(8,128)} fusion(f32[8,512,256]{2,1,0:T(8,128)} %get-tuple-element.730, s32[]{:T(128)} %get-tuple-element.729, bf16[2048,256]{1,0:T(8,128)(2,1)} %get-tuple-element.764, f32[64,8,16,128]{3,2,1,0:T(8,128)} %bitcast.68, bf16[2048,768]{1,0:T(8,128)(2,1)S(1)} %get-tuple-element.760, f32[2048]{0:T(1024)S(1)} %get-tuple-element.763, ...), kind=kOutput, calls=%fused_computation.28.clone.1 | convolution fusion | flops 2162163712 | bytes 9740804 | tf_op jit(solution)/shard_map/while/body/eval_jaxpr/dot_general | solution.py:99
  346.9 0.6 dynamic_slice.132
  350.0 2.4 broadcast_in_dim.66
  353.9 7.6 %fusion.83 = f32[8,512,256]{2,1,0:T(8,128)} fusion(f32[8,512,256]{2,1,0:T(8,128)} %get-tuple-element.730, s32[]{:T(128)} %get-tuple-element.729, bf16[2048,256]{1,0:T(8,128)(2,1)} %get-tuple-element.764, f32[64,8,16,128]{3,2,1,0:T(8,128)} %bitcast.68, bf16[2048,768]{1,0:T(8,128)(2,1)S(1)} %get-tuple-element.760, f32[2048]{0:T(1024)S(1)} %get-tuple-element.763, ...), kind=kOutput, calls=%fused_computation.28.clone.1 | convolution fusion | flops 2162163712 | bytes 9740804 | tf_op jit(solution)/shard_map/while/body/eval_jaxpr/dot_general | solution.py:99
  361.6 0.6 dynamic_slice.132
  364.7 2.4 broadcast_in_dim.66
  368.6 7.6 %fusion.83 = f32[8,512,256]{2,1,0:T(8,128)} fusion(f32[8,512,256]{2,1,0:T(8,128)} %get-tuple-element.730, s32[]{:T(128)} %get-tuple-element.729, bf16[2048,256]{1,0:T(8,128)(2,1)} %get-tuple-element.764, f32[64,8,16,128]{3,2,1,0:T(8,128)} %bitcast.68, bf16[2048,768]{1,0:T(8,128)(2,1)S(1)} %get-tuple-element.760, f32[2048]{0:T(1024)S(1)} %get-tuple-element.763, ...), kind=kOutput, calls=%fused_computation.28.clone.1 | convolution fusion | flops 2162163712 | bytes 9740804 | tf_op jit(solution)/shard_map/while/body/eval_jaxpr/dot_general | solution.py:99
  376.2 0.6 dynamic_slice.132
  379.3 2.4 broadcast_in_dim.66
  383.2 7.6 %fusion.83 = f32[8,512,256]{2,1,0:T(8,128)} fusion(f32[8,512,256]{2,1,0:T(8,128)} %get-tuple-element.730, s32[]{:T(128)} %get-tuple-element.729, bf16[2048,256]{1,0:T(8,128)(2,1)} %get-tuple-element.764, f32[64,8,16,128]{3,2,1,0:T(8,128)} %bitcast.68, bf16[2048,768]{1,0:T(8,128)(2,1)S(1)} %get-tuple-element.760, f32[2048]{0:T(1024)S(1)} %get-tuple-element.763, ...), kind=kOutput, calls=%fused_computation.28.clone.1 | convolution fusion | flops 2162163712 | bytes 9740804 | tf_op jit(solution)/shard_map/while/body/eval_jaxpr/dot_general | solution.py:99
  390.8 0.6 dynamic_slice.132
  393.8 2.4 broadcast_in_dim.66
  397.7 7.6 %fusion.83 = f32[8,512,256]{2,1,0:T(8,128)} fusion(f32[8,512,256]{2,1,0:T(8,128)} %get-tuple-element.730, s32[]{:T(128)} %get-tuple-element.729, bf16[2048,256]{1,0:T(8,128)(2,1)} %get-tuple-element.764, f32[64,8,16,128]{3,2,1,0:T(8,128)} %bitcast.68, bf16[2048,768]{1,0:T(8,128)(2,1)S(1)} %get-tuple-element.760, f32[2048]{0:T(1024)S(1)} %get-tuple-element.763, ...), kind=kOutput, calls=%fused_computation.28.clone.1 | convolution fusion | flops 2162163712 | bytes 9740804 | tf_op jit(solution)/shard_map/while/body/eval_jaxpr/dot_general | solution.py:99
  405.4 0.6 dynamic_slice.132
  408.5 2.4 broadcast_in_dim.66
  412.4 7.6 %fusion.83 = f32[8,512,256]{2,1,0:T(8,128)} fusion(f32[8,512,256]{2,1,0:T(8,128)} %get-tuple-element.730, s32[]{:T(128)} %get-tuple-element.729, bf16[2048,256]{1,0:T(8,128)(2,1)} %get-tuple-element.764, f32[64,8,16,128]{3,2,1,0:T(8,128)} %bitcast.68, bf16[2048,768]{1,0:T(8,128)(2,1)S(1)} %get-tuple-element.760, f32[2048]{0:T(1024)S(1)} %get-tuple-element.763, ...), kind=kOutput, calls=%fused_computation.28.clone.1 | convolution fusion | flops 2162163712 | bytes 9740804 | tf_op jit(solution)/shard_map/while/body/eval_jaxpr/dot_general | solution.py:99
  420.0 0.6 dynamic_slice.132
  423.1 2.4 broadcast_in_dim.66
  427.0 7.6 %fusion.83 = f32[8,512,256]{2,1,0:T(8,128)} fusion(f32[8,512,256]{2,1,0:T(8,128)} %get-tuple-element.730, s32[]{:T(128)} %get-tuple-element.729, bf16[2048,256]{1,0:T(8,128)(2,1)} %get-tuple-element.764, f32[64,8,16,128]{3,2,1,0:T(8,128)} %bitcast.68, bf16[2048,768]{1,0:T(8,128)(2,1)S(1)} %get-tuple-element.760, f32[2048]{0:T(1024)S(1)} %get-tuple-element.763, ...), kind=kOutput, calls=%fused_computation.28.clone.1 | convolution fusion | flops 2162163712 | bytes 9740804 | tf_op jit(solution)/shard_map/while/body/eval_jaxpr/dot_general | solution.py:99
  434.6 0.6 dynamic_slice.132
  437.7 2.4 broadcast_in_dim.66
  441.6 7.6 %fusion.83 = f32[8,512,256]{2,1,0:T(8,128)} fusion(f32[8,512,256]{2,1,0:T(8,128)} %get-tuple-element.730, s32[]{:T(128)} %get-tuple-element.729, bf16[2048,256]{1,0:T(8,128)(2,1)} %get-tuple-element.764, f32[64,8,16,128]{3,2,1,0:T(8,128)} %bitcast.68, bf16[2048,768]{1,0:T(8,128)(2,1)S(1)} %get-tuple-element.760, f32[2048]{0:T(1024)S(1)} %get-tuple-element.763, ...), kind=kOutput, calls=%fused_computation.28.clone.1 | convolution fusion | flops 2162163712 | bytes 9740804 | tf_op jit(solution)/shard_map/while/body/eval_jaxpr/dot_general | solution.py:99
  449.2 133.0 %all-reduce.2.cloned.1.call-done = f32[4096,256]{1,0:T(8,128)} async-done(((f32[4096,256]{1,0:T(8,128)}), f32[4096,256]{1,0:T(8,128)}) %all-reduce.2.cloned.1.call-update) | async-done | bytes 4194320 | tf_op jit(solution)/shard_map/psum | solution.py:103
  582.2 1.7 constant_dynamic-slice_fusion.2
  (128 shorter events, 5.9 us)
Async XLA Ops:
  6.5 150.3 %all-gather.6.cloned.1.call-start = ((), (), s32[]{:S(2)}) async-start(), calls=%async_computation.1 | async-start | bytes 3538944 | tf_op jit(solution)/shard_map/all_gather | solution.py:41
  11.5 8.1 %copy-start.3 = (bf16[256]{0:T(256)(128)(2,1)S(1)}, bf16[256]{0:T(256)(128)(2,1)}, u32[]{:S(2)}) copy-start(bf16[256]{0:T(256)(128)(2,1)} %param.10) | copy-start | bytes 1540
  11.5 144.6 %copy-start.2 = (s32[256]{0:T(256)S(1)}, s32[256]{0:T(256)}, u32[]{:S(2)}) copy-start(s32[256]{0:T(256)} %param.12) | copy-start | bytes 3076
  11.5 145.0 %copy-start.1 = (s32[64,64]{1,0:T(8,128)S(1)}, s32[64,64]{1,0:T(8,128)}, u32[]{:S(2)}) copy-start(s32[64,64]{1,0:T(8,128)} %param.13) | copy-start | bytes 49156
  11.5 148.1 %all-to-all-start = ((bf16[16,256,768]{2,1,0:T(8,128)(2,1)}), bf16[16,256,768]{2,1,0:T(8,128)(2,1)}, u32[]{:S(2)}, u32[]{:S(2)}) async-start(bf16[16,256,768]{2,1,0:T(8,128)(2,1)} %stack.2), calls=%async_computation | async-start | bytes 12582912 | tf_op jit(solution)/shard_map/all_to_all | solution.py:33
  18.6 313.8 %all-gather.8.cloned.1.call-start = ((), (), s32[]{:S(2)}) async-start(), calls=%async_computation.2 | async-start | bytes 1179648 | tf_op jit(solution)/shard_map/all_gather | solution.py:43
  19.3 562.9 %all-reduce.2.cloned.1.call-start = ((), (), s32[]{:S(2)}) async-start(), calls=%async_computation.3 | async-start | bytes 8388608 | tf_op jit(solution)/shard_map/psum | solution.py:103
  156.9 6.9 %copy-start = (bf16[2048,768]{1,0:T(8,128)(2,1)S(1)}, bf16[2048,768]{1,0:T(8,128)(2,1)}, u32[]{:S(2)}) copy-start(bf16[2048,768]{1,0:T(8,128)(2,1)} %all-gather.6.cloned.1.call-done) | copy-start | bytes 9437188
Sparse Core Ops, SparseCore 0:
  9.7 87.4 all-gather.5
  99.5 44.2 all-gather.7
  449.3 132.8 all-reduce.1
